TPU v7x, 256 devices: a whole 4x4x8 slice. The times are simulated.
256 devices in a mesh: row: 8 (over z_hi, core), col: 32 (over y, z_lo, x).
Axes of the slice: x: 4, y: 4, z: 8 (z_hi: 4, z_lo: 2; z = z_hi * 2 + z_lo), core: 2. Of those that a mesh axis runs over, the one named last changes fastest.
Arguments:
- features: bfloat16 [65536, 512], P('col'), may hold values from -6 to 6
- weight_raw: bfloat16 [512, 512], P('col'), may hold values from -0.0234375 to 0.0234375
- direction_raw: bfloat16 [512, 512], P('col'), may hold values from -0.0014648438 to 0.0014648438
- panel_index: int32 [4096], P('row'), may hold values from 0 to 65535, as said below
- labels: int32 [4096, 65536], P('row', 'col'), may hold values 0 or 1
Outputs:
- gradient: float32 [512, 512], P('col')
- hess_vec: float32 [512, 512], P('col')
Inputs may be any that keep to these rules, and one draw needn't show every extreme that they name: `panel_index`: distinct compounds; the largest entry is 65535.
All inputs are finite; a program needn't handle non-finite values. No bound on the sum of `labels` on one device may be relied on, other than what follows from the above.
Results may differ from a plain program's by a relative error of at most 0.0033.
Values may be sent and summed in bfloat16 or wider, within the bound.
No kernel may reach another device: no remote copies, remote signals or barrier semaphores. Data moves between devices by JAX's collectives and lax.ppermute only.
A program may use at most 64 MiB of HBM per device.

v0:
```python
import math
import jax
import jax.numpy as jnp
from jax import lax
from jax.sharding import PartitionSpec as P


def symmetric(matrix):
    as_float = matrix.astype(jnp.float32)
    return ((as_float + as_float.T) * 0.5).astype(jnp.bfloat16)


def shards(features, weight_raw, direction_raw, panel_index, labels):
    weight_full, direction_full = (
        lax.all_gather(weight_raw, "col", axis=0, tiled=True),
        lax.all_gather(direction_raw, "col", axis=0, tiled=True),
    )
    weight_sym = symmetric(weight_full)
    direction_sym = symmetric(direction_full)
    col_count = features.shape[0]
    offset = lax.axis_index("col") * col_count
    local_pos = panel_index - offset
    is_owned = (local_pos >= 0) & (local_pos < col_count)
    picked = jnp.take(features, jnp.clip(local_pos, 0, col_count - 1), axis=0)
    picked = jnp.where(is_owned[:, None], picked.astype(jnp.float32), 0.0)
    panel_rows = lax.psum(picked.astype(jnp.bfloat16), "col")
    panel_count = panel_rows.shape[0]
    proj_weight = jnp.dot(panel_rows, weight_sym, preferred_element_type=jnp.float32)
    proj_direction = jnp.dot(panel_rows, direction_sym, preferred_element_type=jnp.float32)
    projected = jnp.concatenate([proj_weight, proj_direction], axis=0).astype(jnp.bfloat16)
    pair_vals = lax.dot_general(
        projected, features, (((1,), (1,)), ((), ())), preferred_element_type=jnp.float32
    )
    margin = pair_vals[:panel_count]
    change = pair_vals[panel_count:]
    probability = jax.nn.sigmoid(margin)
    residual_weight = probability - labels.astype(jnp.float32)
    curvature_weight = probability * (1.0 - probability) * change
    pair_weights = jnp.concatenate([residual_weight, curvature_weight], axis=0).astype(jnp.bfloat16)
    col_sums = jnp.dot(pair_weights, features, preferred_element_type=jnp.float32)
    resid_sums = col_sums[:panel_count]
    curv_sums = col_sums[panel_count:]
    panel_float = panel_rows.astype(jnp.float32)
    pair_scale = 1.0 / math.sqrt(
        panel_count * lax.axis_size("row") * col_count * lax.axis_size("col")
    )
    highest = lax.Precision.HIGHEST
    grad_half = jnp.dot(
        panel_float.T, resid_sums, preferred_element_type=jnp.float32, precision=highest
    )
    curv_half = jnp.dot(
        panel_float.T, curv_sums, preferred_element_type=jnp.float32, precision=highest
    )
    grad_term = (grad_half + grad_half.T) * (0.5 * pair_scale)
    curv_term = (curv_half + curv_half.T) * (0.5 * pair_scale)
    summed = lax.psum((grad_term, curv_term), "row")
    gradient, hess_vec = (
        lax.psum_scatter(summed[0], "col", scatter_dimension=0, tiled=True),
        lax.psum_scatter(summed[1], "col", scatter_dimension=0, tiled=True),
    )
    return (gradient, hess_vec)


def solution(mesh):
    return jax.shard_map(
        shards,
        mesh=mesh,
        in_specs=(P("col", None), P("col", None), P("col", None), P("row"), P("row", "col")),
        out_specs=(P("col", None), P("col", None)),
        check_vma=False,
    )
```

profile of v0, /device:TPU:2, one launch (start us, length us, event | category | flops | bytes accessed | tf_op | source)
XLA Modules:
  0.0 745.7 jit_solution(11462926430872568928)
XLA Ops:
  7.2 0.0 copy-start
  7.2 0.0 all-reduce.4.cloned.1.call-start
  7.2 0.8 compare_and_fusion
  8.1 0.7 copy-done
  8.8 0.0 copy-start.5
  8.8 2.0 gather_fusion
  10.8 1.0 select_convert_fusion
  11.8 0.0 copy-start.6
  11.8 0.0 all-reduce.4.cloned.1.call-update
  11.8 0.0 reduce-scatter.3.cloned.1.call-start
  11.8 0.0 copy-done.5
  11.8 80.4 %all_gather.7 = bf16[512,512]{1,0:T(8,128)(2,1)S(1)} all-gather(bf16[16,512]{1,0:T(8,128)(2,1)S(1)} %copy-done.5), channel_id=1, replica_groups=mesh['row'=8,'col'=32] {'col'}, dimensions={0}, use_global_device_ids=true | all-gather | bytes 540672 | tf_op jit(solution)/shard_map/all_gather | solution.py:16
  92.2 0.2 copy.18
  92.4 1.2 copy.19
  93.6 0.0 copy-done.6
  93.6 83.0 %all_gather.6 = bf16[512,512]{1,0:T(8,128)(2,1)S(1)} all-gather(bf16[16,512]{1,0:T(8,128)(2,1)S(1)} %copy-done.6), channel_id=1, replica_groups=mesh['row'=8,'col'=32] {'col'}, dimensions={0}, use_global_device_ids=true | all-gather | bytes 540672 | tf_op jit(solution)/shard_map/all_gather | solution.py:15
  176.6 1.2 copy.17
  177.8 148.2 %all-reduce.4.cloned.1.call-done = bf16[512,512]{1,0:T(8,128)(2,1)} async-done(((bf16[512,512]{1,0:T(8,128)(2,1)}), bf16[512,512]{1,0:T(8,128)(2,1)}) %all-reduce.4.cloned.1.call-update) | async-done | bytes 524304 | tf_op jit(solution)/shard_map/psum | solution.py:26
  326.0 0.0 copy-start.1
  326.0 0.0 copy-start.2
  326.0 2.0 convolution_convert_fusion
  328.0 0.0 copy-done.1
  328.0 0.0 copy-done.2
  328.0 0.5 convolution_convert_fusion.1
  328.5 0.0 copy-start.3
  328.5 2.4 fusion.13
  330.8 0.0 copy-done.3
  330.9 1.7 subtract_convert_fusion
  332.6 2.3 fusion.5
  334.9 0.0 copy-start.4
  334.9 1.3 copy-done.4
  336.3 1.1 fusion.11
  337.4 1.3 copy.20
  338.7 2.4 fusion.18
  341.1 0.0 reduce-scatter.3.cloned.1.call-update
  341.1 0.0 reduce-scatter.5.cloned.1.call-start
  341.2 2.5 fusion.9
  343.7 1.3 copy.21
  345.0 2.4 fusion.17
  347.4 0.0 reduce-scatter.5.cloned.1.call-update
  347.4 0.0 all-reduce.6.cloned.1.call-start
  347.5 152.4 %reduce-scatter.3.cloned.1.call-done = f32[16,512]{1,0:T(8,128)} async-done(((f32[512,512]{1,0:T(8,128)}), f32[16,512]{1,0:T(8,128)}) %reduce-scatter.3.cloned.1.call-update) | async-done | bytes 32784 | tf_op jit(solution)/shard_map/reduce_scatter | solution.py:58
  499.9 161.8 %reduce-scatter.5.cloned.1.call-done = f32[16,512]{1,0:T(8,128)} async-done(((f32[512,512]{1,0:T(8,128)}), f32[16,512]{1,0:T(8,128)}) %reduce-scatter.5.cloned.1.call-update) | async-done | bytes 32784 | tf_op jit(solution)/shard_map/reduce_scatter | solution.py:59
  661.6 0.0 all-reduce.6.cloned.1.call-update
  661.7 74.7 %all-reduce.6.cloned.1.call-done = (f32[16,512]{1,0:T(8,128)}, f32[16,512]{1,0:T(8,128)}) async-done(((f32[16,512]{1,0:T(8,128)}, f32[16,512]{1,0:T(8,128)}), (f32[16,512]{1,0:T(8,128)}, f32[16,512]{1,0:T(8,128)})) %all-reduce.6.cloned.1.call-update) | async-done | bytes 65552 | tf_op jit(solution)/shard_map/psum | solution.py:56
  736.4 1.4 copy.25
  737.8 1.4 copy.26
  (1 shorter events, 0.0 us)
Async XLA Ops:
  7.2 1.6 copy-start
  7.2 318.8 %all-reduce.4.cloned.1.call-start = ((), (), s32[]{:S(2)}) async-start(), calls=%async_computation.2 | async-start | bytes 1048576 | tf_op jit(solution)/shard_map/psum | solution.py:26
  8.8 3.1 copy-start.5
  11.8 81.9 %copy-start.6 = (bf16[16,512]{1,0:T(8,128)(2,1)S(1)}, bf16[16,512]{1,0:T(8,128)(2,1)}, u32[]{:S(2)}) copy-start(bf16[16,512]{1,0:T(8,128)(2,1)} %param.6) | copy-start | bytes 49156
  11.8 488.1 %reduce-scatter.3.cloned.1.call-start = ((), (), s32[]{:S(2)}) async-start(), calls=%async_computation.3 | async-start | bytes 1081344 | tf_op jit(solution)/shard_map/reduce_scatter | solution.py:58
  326.0 2.0 copy-start.1
  326.0 2.0 copy-start.2
  328.5 2.4 copy-start.3
  334.9 1.3 copy-start.4
  341.1 320.5 %reduce-scatter.5.cloned.1.call-start = ((), (), s32[]{:S(2)}) async-start(), calls=%async_computation.4 | async-start | bytes 1081344 | tf_op jit(solution)/shard_map/reduce_scatter | solution.py:59
  347.4 389.0 %all-reduce.6.cloned.1.call-start = ((), (), s32[]{:S(2)}) async-start(), calls=%async_computation.5 | async-start | bytes 131072 | tf_op jit(solution)/shard_map/psum | solution.py:56
Sparse Core Ops, SparseCore 0:
  11.9 314.0 all-reduce.3
  341.3 158.5 reduce-scatter.2
  502.4 159.2 reduce-scatter.4
  664.3 72.0 all-reduce.5
where the time goes:
time: 746 us
  waiting for transfers between devices  537 us (72%)
  blocking collectives  163 us (22%)
  between operations  13.9 us (2%)
  local copies, waits for them, and re-layouts  12 us (2%)
  matrix products  10.7 us (1%)
  other arithmetic  8.43 us (1%)
    reduce_scatter x1, waiting for transfers between devices, shards(): lax.psum_scatter(summed[1], 'col', scatter_dimension=0, tiled=True)  162 us
    reduce_scatter x1, waiting for transfers between devices, shards(): lax.psum_scatter(summed[0], 'col', scatter_dimension=0, tiled=True)  152 us
    psum x1, waiting for transfers between devices, shards(): panel_rows = lax.psum(picked.astype(jnp.bfloat16), 'col')  148 us
    all_gather x1, blocking collectives, shards(): lax.all_gather(weight_raw, 'col', axis=0, tiled=True)  83 us
    all_gather x1, blocking collectives, shards(): lax.all_gather(direction_raw, 'col', axis=0, tiled=True)  80.4 us
    psum x1, waiting for transfers between devices, shards(): summed = lax.psum((grad_term, curv_term), 'row')  74.7 us
  transfers between devices with their start and end apart: 4, of which 4 were waited for; matrix products, arithmetic and copies ran while one was open for 1% of the time, Pallas kernels for 0%

commit v1 on v0

--- a/solution.py
+++ b/solution.py
@@ -23,7 +23,7 @@
     is_owned = (local_pos >= 0) & (local_pos < col_count)
     picked = jnp.take(features, jnp.clip(local_pos, 0, col_count - 1), axis=0)
     picked = jnp.where(is_owned[:, None], picked.astype(jnp.float32), 0.0)
-    panel_rows = lax.psum(picked.astype(jnp.bfloat16), "col")
+    panel_rows = jnp.sum(lax.all_gather(picked.astype(jnp.bfloat16), "col"), axis=0)
     panel_count = panel_rows.shape[0]
     proj_weight = jnp.dot(panel_rows, weight_sym, preferred_element_type=jnp.float32)
     proj_direction = jnp.dot(panel_rows, direction_sym, preferred_element_type=jnp.float32)

time: 746 us -> 648 us (0.87)
  waiting for transfers between devices: 537 us -> 419 us
  other arithmetic: 8.43 us -> 17.6 us
    psum x1 -> x0, waiting for transfers between devices: 148 us -> none  [shards(): panel_rows = lax.psum(picked.astype(jnp.bfloat16), 'col')]
    all_gather x0 -> x1, waiting for transfers between devices: none -> 32 us  [shards(): lax.all_gather(picked.astype(jnp.bfloat16), 'col')]
    reduce_sum x0 -> x1, other arithmetic: none -> 8.8 us  [shards(): jnp.sum(lax.all_gather(picked.astype(jnp.bfloat16), 'col'), axis=0)]
  transfers between devices with their start and end apart: 4 -> 4, of which waited for: 4 -> 4; matrix products, arithmetic and copies ran while one was open for 1% -> 2% of each run, Pallas kernels for 0% -> 0%
where the time goes in v1:
time: 648 us
  waiting for transfers between devices  419 us (65%)
  blocking collectives  170 us (26%)
  other arithmetic  17.6 us (3%)
  between operations  13.9 us (2%)
  matrix products  13.6 us (2%)
  local copies, waits for them, and re-layouts  13.5 us (2%)
    reduce_scatter x1, waiting for transfers between devices, shards(): lax.psum_scatter(summed[1], 'col', scatter_dimension=0, tiled=True)  162 us
    reduce_scatter x1, waiting for transfers between devices, shards(): lax.psum_scatter(summed[0], 'col', scatter_dimension=0, tiled=True)  151 us
    all_gather x1, blocking collectives, shards(): lax.all_gather(weight_raw, 'col', axis=0, tiled=True)  86.5 us
    all_gather x1, blocking collectives, shards(): lax.all_gather(direction_raw, 'col', axis=0, tiled=True)  83.1 us
    psum x1, waiting for transfers between devices, shards(): summed = lax.psum((grad_term, curv_term), 'row')  74.5 us
    all_gather x1, waiting for transfers between devices, shards(): lax.all_gather(picked.astype(jnp.bfloat16), 'col')  32 us
  transfers between devices with their start and end apart: 4, of which 4 were waited for; matrix products, arithmetic and copies ran while one was open for 2% of the time, Pallas kernels for 0%

profile of v1, /device:TPU:2, one launch (start us, length us, event | category | flops | bytes accessed | tf_op | source)
XLA Modules:
  0.0 647.7 jit_solution(14447671436594955789)
XLA Ops:
  7.2 0.0 copy-start
  7.2 0.0 copy-start.4
  7.2 0.0 all-gather.2.cloned.1.call-start
  7.2 0.8 compare_and_fusion
  8.1 0.7 copy-done
  8.8 0.0 copy-start.5
  8.8 2.0 gather_fusion
  10.8 1.0 select_convert_fusion
  11.8 0.0 all-gather.2.cloned.1.call-update
  11.8 0.0 reduce-scatter.3.cloned.1.call-start
  11.8 0.0 copy-done.4
  11.8 83.1 %all_gather.12 = bf16[512,512]{1,0:T(8,128)(2,1)S(1)} all-gather(bf16[16,512]{1,0:T(8,128)(2,1)S(1)} %copy-done.4), channel_id=1, replica_groups=mesh['row'=8,'col'=32] {'col'}, dimensions={0}, use_global_device_ids=true | all-gather | bytes 540672 | tf_op jit(solution)/shard_map/all_gather | solution.py:16
  94.9 0.2 copy.18
  95.1 1.2 copy.19
  96.3 0.0 copy-done.5
  96.3 86.5 %all_gather.11 = bf16[512,512]{1,0:T(8,128)(2,1)S(1)} all-gather(bf16[16,512]{1,0:T(8,128)(2,1)S(1)} %copy-done.5), channel_id=1, replica_groups=mesh['row'=8,'col'=32] {'col'}, dimensions={0}, use_global_device_ids=true | all-gather | bytes 540672 | tf_op jit(solution)/shard_map/all_gather | solution.py:15
  182.8 0.0 copy-start.1
  182.8 1.2 copy.17
  184.0 0.0 copy-done.1
  184.0 32.0 %all-gather.2.cloned.1.call-done = bf16[32,512,512]{2,1,0:T(8,128)(2,1)} async-done(((bf16[1,512,512]{2,1,0:T(8,128)(2,1)}), bf16[32,512,512]{2,1,0:T(8,128)(2,1)}) %all-gather.2.cloned.1.call-update) | async-done | bytes 16777232 | tf_op jit(solution)/shard_map/all_gather | solution.py:26
  216.0 8.8 %reduce_sum.12 = bf16[512,512]{1,0:T(8,128)(2,1)S(1)} reduce(bf16[32,512,512]{2,1,0:T(8,128)(2,1)} %all-gather.2.cloned.1.call-done, bf16[]{:T(256)} %constant.16.clone.1), dimensions={0}, to_apply=%region_0.1 | reduce | flops 8126464 | bytes 17301506 | tf_op jit(solution)/shard_map/reduce_sum | solution.py:26
  224.8 1.7 convolution_convert_fusion
  226.5 1.8 convolution_convert_fusion.1
  228.3 0.0 copy-start.2
  228.3 2.4 fusion.13
  230.7 0.0 copy-done.2
  230.7 1.7 subtract_convert_fusion
  232.5 2.3 fusion.5
  234.8 0.0 copy-start.3
  234.8 1.3 copy-done.3
  236.1 2.1 fusion.11
  238.2 2.5 copy.20
  240.8 2.8 fusion.18
  243.5 0.0 reduce-scatter.3.cloned.1.call-update
  243.5 0.0 reduce-scatter.5.cloned.1.call-start
  243.6 3.3 fusion.9
  246.9 1.6 copy.21
  248.5 2.4 fusion.17
  250.9 0.0 reduce-scatter.5.cloned.1.call-update
  250.9 0.0 all-reduce.3.cloned.1.call-start
  251.0 151.0 %reduce-scatter.3.cloned.1.call-done = f32[16,512]{1,0:T(8,128)} async-done(((f32[512,512]{1,0:T(8,128)}), f32[16,512]{1,0:T(8,128)}) %reduce-scatter.3.cloned.1.call-update) | async-done | bytes 32784 | tf_op jit(solution)/shard_map/reduce_scatter | solution.py:58
  402.0 161.9 %reduce-scatter.5.cloned.1.call-done = f32[16,512]{1,0:T(8,128)} async-done(((f32[512,512]{1,0:T(8,128)}), f32[16,512]{1,0:T(8,128)}) %reduce-scatter.5.cloned.1.call-update) | async-done | bytes 32784 | tf_op jit(solution)/shard_map/reduce_scatter | solution.py:59
  563.9 0.0 all-reduce.3.cloned.1.call-update
  563.9 74.5 %all-reduce.3.cloned.1.call-done = (f32[16,512]{1,0:T(8,128)}, f32[16,512]{1,0:T(8,128)}) async-done(((f32[16,512]{1,0:T(8,128)}, f32[16,512]{1,0:T(8,128)}), (f32[16,512]{1,0:T(8,128)}, f32[16,512]{1,0:T(8,128)})) %all-reduce.3.cloned.1.call-update) | async-done | bytes 65552 | tf_op jit(solution)/shard_map/psum | solution.py:56
  638.4 1.4 copy.24
  639.8 1.4 copy.25
  (1 shorter events, 0.0 us)
Async XLA Ops:
  7.2 1.6 copy-start
  7.2 4.7 copy-start.4
  7.2 208.8 %all-gather.2.cloned.1.call-start = ((), (), s32[]{:S(2)}) async-start(), calls=%async_computation.2 | async-start | bytes 17301504 | tf_op jit(solution)/shard_map/all_gather | solution.py:26
  8.8 87.5 %copy-start.5 = (bf16[16,512]{1,0:T(8,128)(2,1)S(1)}, bf16[16,512]{1,0:T(8,128)(2,1)}, u32[]{:S(2)}) copy-start(bf16[16,512]{1,0:T(8,128)(2,1)} %param.6) | copy-start | bytes 49156
  11.8 390.2 %reduce-scatter.3.cloned.1.call-start = ((), (), s32[]{:S(2)}) async-start(), calls=%async_computation.3 | async-start | bytes 1081344 | tf_op jit(solution)/shard_map/reduce_scatter | solution.py:58
  182.8 1.2 copy-start.1
  228.3 2.4 copy-start.2
  234.8 1.3 copy-start.3
  243.5 320.4 %reduce-scatter.5.cloned.1.call-start = ((), (), s32[]{:S(2)}) async-start(), calls=%async_computation.4 | async-start | bytes 1081344 | tf_op jit(solution)/shard_map/reduce_scatter | solution.py:59
  250.9 387.5 %all-reduce.3.cloned.1.call-start = ((), (), s32[]{:S(2)}) async-start(), calls=%async_computation.5 | async-start | bytes 131072 | tf_op jit(solution)/shard_map/psum | solution.py:56
Sparse Core Ops, SparseCore 0:
  11.9 204.0 all-gather.1
  243.7 158.2 reduce-scatter.2
  404.7 159.2 reduce-scatter.4
  566.4 71.9 all-reduce.2
